TPU v7x, 32 devices: a whole 2x2x4 slice. The times are simulated.
32 devices in a mesh: groups: 2 (over y), expert: 4 (over x, core), hidden: 4 (over z).
Axes of the slice: x: 2, y: 2, z: 4, core: 2. Of those that a mesh axis runs over, the one named last changes fastest.
Arguments:
- tokens: bfloat16 [1024, 3072], P(('groups', 'expert'), 'hidden'), parts along dimension 0, may hold values from -6 to 6
- routes: int32 [1024, 2], P(('groups', 'expert')), parts along dimension 0, may hold values from 0 to 7, all different within a row; in each aligned block of 128 rows (0 to 127, 128 to 255, ...) at most 48 rows name the same one
- router_weight: bfloat16 [3072, 8], replicated, may hold values from -0.109375 to 0.109375
- gate_weight: bfloat16 [8, 3072, 8192], P('expert', None, 'hidden'), may hold values from -0.109375 to 0.109375
- up_weight: bfloat16 [8, 3072, 8192], P('expert', None, 'hidden'), may hold values from -0.109375 to 0.109375
- down_weight: bfloat16 [8, 8192, 3072], P('expert', 'hidden'), may hold values from -0.09375 to 0.09375
Outputs:
- mixed: bfloat16 [1024, 3072], P(('groups', 'expert'), 'hidden'), parts along dimension 0
There are 2 independent parts, one for each index of `groups`. A program takes and returns all parts, laid end to end along the dimension named above; an argument that names none is the same for every part. Nothing has to cross between parts.
Inputs may be any that keep to these rules, and one draw needn't show every extreme that they name: `routes`: each token names two different experts. Among the 128 tokens of one index of expert (aligned blocks of rows) no expert is named more than 48 times, a bound that some block reaches.
All inputs are finite; a program needn't handle non-finite values.
Results may differ from a plain program's by a relative error of at most 0.0057.
Values may be sent and summed in bfloat16 or wider, within the bound.
No kernel may reach another device: no remote copies, remote signals or barrier semaphores. Data moves between devices by JAX's collectives and lax.ppermute only.
A program may use at most 128 MiB of HBM per device.

v0:
```python
import jax
import jax.numpy as jnp
from jax import lax
from jax.sharding import PartitionSpec as P

CAP = 48


def per_device(tokens, routes, router_weight, gate_weight, up_weight, down_weight):
    experts_here = gate_weight.shape[0]
    groups = lax.axis_size("expert")
    experts_all = experts_here * groups
    local_tokens = tokens.shape[0]
    capacity = CAP
    flat_ids = routes.reshape(-1)
    onehot = (flat_ids[:, None] == jnp.arange(experts_all, dtype=jnp.int32)[None, :]).astype(
        jnp.int32
    )
    position = jnp.sum((jnp.cumsum(onehot, axis=0) - onehot) * onehot, axis=1)
    slot_of = flat_ids * capacity + position
    owners = jnp.arange(flat_ids.shape[0], dtype=jnp.int32) // 2
    inverse = jnp.full((experts_all * capacity,), local_tokens, jnp.int32).at[slot_of].set(owners)
    gathered = lax.all_gather(tokens, "hidden", axis=1, tiled=True)
    logits = jnp.dot(gathered, router_weight, preferred_element_type=jnp.float32)
    padded = jnp.concatenate([gathered, jnp.zeros((1, gathered.shape[1]), jnp.bfloat16)], axis=0)
    send_rows = padded[inverse].reshape(experts_all, 1, capacity, gathered.shape[1])
    arrived = lax.all_to_all(send_rows, "expert", split_axis=0, concat_axis=1, tiled=True)
    gate_act = jnp.einsum(
        "ensd,edf->ensf", arrived, gate_weight, preferred_element_type=jnp.float32
    )
    up_act = jnp.einsum("ensd,edf->ensf", arrived, up_weight, preferred_element_type=jnp.float32)
    hidden_act = (jax.nn.silu(gate_act) * up_act).astype(jnp.bfloat16)
    hidden_act = hidden_act.reshape(experts_here, groups * capacity, hidden_act.shape[3])
    partial_value = jnp.einsum(
        "erf,efd->erd", hidden_act, down_weight, preferred_element_type=jnp.float32
    )
    summed = lax.psum_scatter(partial_value, "hidden", scatter_dimension=2, tiled=True).astype(
        jnp.bfloat16
    )
    summed = summed.reshape(experts_here, groups, capacity, summed.shape[2])
    returned = lax.all_to_all(summed, "expert", split_axis=1, concat_axis=0, tiled=True)
    results = returned.reshape(experts_all * capacity, returned.shape[3])
    selected = jnp.take_along_axis(logits, routes, axis=1)
    share = jax.nn.sigmoid(selected[:, 0] - selected[:, 1])
    slot_pairs = slot_of.reshape(local_tokens, 2)
    first_out = results[slot_pairs[:, 0]].astype(jnp.float32)
    second_out = results[slot_pairs[:, 1]].astype(jnp.float32)
    mixture = share[:, None] * first_out + (1.0 - share)[:, None] * second_out
    return mixture.astype(jnp.bfloat16)


def solution(mesh):
    return jax.shard_map(
        per_device,
        mesh=mesh,
        in_specs=(
            P(("groups", "expert"), "hidden"),
            P(("groups", "expert"), None),
            P(),
            P("expert", None, "hidden"),
            P("expert", None, "hidden"),
            P("expert", "hidden", None),
        ),
        out_specs=P(("groups", "expert"), "hidden"),
        check_vma=False,
    )
```

profile of v0, /device:TPU:0, one launch (start us, length us, event | category | flops | bytes accessed | tf_op | source)
XLA Modules:
  0.0 209.8 jit_solution(10546477326377145028)
XLA Ops:
  6.5 0.8 copy.41
  7.3 0.1 eq.29
  7.5 0.1 eq.25
  7.6 0.6 reduce-window.6
  8.2 0.2 slice_reduce_fusion
  8.5 0.1 fusion.13
  8.6 0.1 reduce_sum.15
  8.7 0.1 mul.51
  8.9 1.4 scatter_custom_fusion
  10.3 21.5 %all_gather.3 = bf16[128,3072]{1,0:T(8,128)(2,1)S(1)} all-gather(bf16[128,768]{1,0:T(8,128)(2,1)} %param.6), channel_id=1, replica_groups=mesh['groups'=2,'expert'=4,'hidden'=4] {'hidden'}, dimensions={1}, use_global_device_ids=true | all-gather | bytes 983040 | tf_op jit(solution)/shard_map/all_gather | solution.py:23
  31.8 0.9 copy-done.1
  32.8 2.9 %gather_fusion = bf16[384,3072]{1,0:T(8,128)(2,1)S(1)} fusion(bf16[129,3072]{1,0:T(8,128)(2,1)S(1)} %concatenate.3, s32[1024]{0:T(1024)S(1)} %pad_clamp_fusion.2), kind=kCustom, calls=%fused_computation | custom fusion | bytes 4720128 | tf_op jit(solution)/shard_map/gather | solution.py:26
  35.7 31.0 %all_to_all.33 = bf16[8,1,48,3072]{3,2,1,0:T(8,128)(2,1)S(1)} all-to-all(bf16[8,1,48,3072]{3,2,1,0:T(8,128)(2,1)S(1)} %bitcast.57), channel_id=1, replica_groups=mesh['groups'=2,'expert'=4,'hidden'=4] {'expert'}, dimensions={0} | all-to-all | bytes 4718592 | tf_op jit(solution)/shard_map/all_to_all | solution.py:27
  66.7 10.8 %fusion.2 = f32[2,4,48,2048]{3,2,1,0:T(8,128)S(1)} fusion(bf16[2,3072,2048]{2,1,0:T(8,128)(2,1)} %param.9, bf16[4,2,1,48,3072]{4,3,1,0,2:T(8,128)(2,1)S(1)} %bitcast.52), kind=kOutput, calls=%fused_computation.7 | convolution fusion | flops 4831838208 | bytes 30670848 | tf_op jit(solution)/shard_map/ensd,edf->ensf/dot_general | solution.py:28
  77.5 11.0 %multiply_convert_fusion = bf16[2,4,48,2048]{3,2,1,0:T(8,128)(2,1)S(1)} fusion(f32[2,4,48,2048]{3,2,1,0:T(8,128)S(1)} %fusion.2, bf16[2,3072,2048]{2,1,0:T(8,128)(2,1)} %param.10, bf16[4,2,1,48,3072]{4,3,1,0,2:T(8,128)(2,1)S(1)} %bitcast.53), kind=kOutput, calls=%fused_computation.9 | convolution fusion | flops 4836556800 | bytes 32243712 | tf_op jit(solution)/shard_map/ensd,edf->ensf/dot_general | solution.py:31
  88.5 12.9 %fusion.19 = f32[2,192,3072]{2,1,0:T(8,128)} fusion(bf16[2,192,2048]{2,1,0:T(8,128)(2,1)S(1)} %bitcast.56, bf16[2,2048,3072]{2,1,0:T(8,128)(2,1)} %param.11), kind=kOutput, calls=%fused_computation.45 | convolution fusion | flops 4831838208 | bytes 31457280 | tf_op jit(solution)/shard_map/erf,efd->erd/dot_general | solution.py:34
  101.5 0.7 copy-done.3
  102.1 0.1 copy.39
  102.2 0.1 reshape.100
  102.4 0.2 copy-done.2
  102.6 0.3 fusion.18
  102.9 1.4 gather_fusion.3
  104.3 0.1 reshape.103
  104.5 0.2 fusion.10
  104.7 80.6 %reduce-scatter.2.cloned.1.call-done = f32[2,192,768]{2,1,0:T(8,128)} async-done(((f32[2,192,3072]{2,1,0:T(8,128)}), f32[2,192,768]{2,1,0:T(8,128)}) %reduce-scatter.2.cloned.1.call-update) | async-done | bytes 1179664 | tf_op jit(solution)/shard_map/reduce_scatter | solution.py:37
  185.3 1.3 convert_element_type.25
  186.6 0.8 copy.46
  187.5 3.5 %all-to-all-start.1 = ((bf16[2,4,48,768]{3,2,0,1:T(8,128)(2,1)}), bf16[2,4,48,768]{3,2,0,1:T(8,128)(2,1)S(1)}, u32[]{:S(2)}, u32[]{:S(2)}) async-start(bf16[2,4,48,768]{3,2,0,1:T(8,128)(2,1)} %copy.46), calls=%async_computation.2 | async-start | bytes 1179648 | tf_op jit(solution)/shard_map/all_to_all | solution.py:41
  191.0 9.5 %all-to-all-done.1 = bf16[2,4,48,768]{3,2,0,1:T(8,128)(2,1)S(1)} async-done(((bf16[2,4,48,768]{3,2,0,1:T(8,128)(2,1)}), bf16[2,4,48,768]{3,2,0,1:T(8,128)(2,1)S(1)}, u32[]{:S(2)}, u32[]{:S(2)}) %all-to-all-start.1) | async-done | bytes 589856 | tf_op jit(solution)/shard_map/all_to_all | solution.py:41
  200.4 0.9 gather_fusion.2
  201.3 0.9 gather_fusion.1
  202.2 0.8 add_convert_fusion
  (21 shorter events, 0.3 us)
Async XLA Ops:
  6.5 95.8 %copy-start = (bf16[3072,8]{0,1:T(8,128)(2,1)S(1)}, bf16[3072,8]{0,1:T(8,128)(2,1)}, u32[]{:S(2)}) copy-start(bf16[3072,8]{0,1:T(8,128)(2,1)} %param.8) | copy-start | bytes 147460
  6.5 178.8 %reduce-scatter.2.cloned.1.call-start = ((), (), s32[]{:S(2)}) async-start(), calls=%async_computation.3 | async-start | bytes 5898240 | tf_op jit(solution)/shard_map/reduce_scatter | solution.py:37
  31.8 0.9 copy-start.1
  101.4 0.7 copy-start.3
  101.4 1.1 copy-start.2
  187.5 13.0 %all-to-all-start.1 = ((bf16[2,4,48,768]{3,2,0,1:T(8,128)(2,1)}), bf16[2,4,48,768]{3,2,0,1:T(8,128)(2,1)S(1)}, u32[]{:S(2)}, u32[]{:S(2)}) async-start(bf16[2,4,48,768]{3,2,0,1:T(8,128)(2,1)} %copy.46), calls=%async_computation.2 | async-start | bytes 1179648 | tf_op jit(solution)/shard_map/all_to_all | solution.py:41
Sparse Core Ops, SparseCore 0:
  101.6 83.6 reduce-scatter.1
where the time goes:
time: 210 us
  waiting for transfers between devices  90.1 us (43%)
  blocking collectives  52.6 us (25%)
  matrix products  35 us (17%)
  between operations  13.6 us (6%)
  local copies, waits for them, and re-layouts  12.1 us (6%)
  starting transfers between devices  3.48 us (2%)
  other arithmetic  3.13 us (1%)
    reduce_scatter x1, waiting for transfers between devices, per_device(): lax.psum_scatter(partial_value, 'hidden', scatter_dimension=2, tiled=True)  80.6 us
    all_to_all x1, blocking collectives, per_device(): lax.all_to_all(send_rows, 'expert', split_axis=0, concat_axis=1, tiled=True)  31 us
    all_gather x1, blocking collectives, per_device(): gathered = lax.all_gather(tokens, 'hidden', axis=1, tiled=True)  21.5 us
    dot_general x1, matrix products, per_device(): jnp.einsum('erf,efd->erd', hidden_act, down_weight, preferred_element_typ...  12.9 us
    dot_general x1, matrix products, per_device(): jnp.einsum('ensd,edf->ensf', arrived, up_weight, preferred_element_type=j...  11 us
    dot_general x1, matrix products, per_device(): jnp.einsum('ensd,edf->ensf', arrived, gate_weight, preferred_element_type...  10.8 us
    all_to_all x1, waiting for transfers between devices, per_device(): lax.all_to_all(summed, 'expert', split_axis=1, concat_axis=0, tiled=True)  9.45 us
  transfers between devices with their start and end apart: 2, of which 2 were waited for; matrix products, arithmetic and copies ran while one was open for 1% of the time, Pallas kernels for 0%

commit v1 on v0

--- a/solution.py
+++ b/solution.py
@@ -20,7 +20,14 @@
     slot_of = flat_ids * capacity + position
     owners = jnp.arange(flat_ids.shape[0], dtype=jnp.int32) // 2
     inverse = jnp.full((experts_all * capacity,), local_tokens, jnp.int32).at[slot_of].set(owners)
-    gathered = lax.all_gather(tokens, "hidden", axis=1, tiled=True)
+    ring = [tokens]
+    for hop in range(3):
+        ring.append(lax.ppermute(ring[-1], "hidden", [(dev, (dev + 1) % 4) for dev in range(4)]))
+    gathered = jnp.roll(
+        jnp.concatenate(ring[::-1], axis=1),
+        (lax.axis_index("hidden") + 1) * ring[0].shape[1],
+        axis=1,
+    )
     logits = jnp.dot(gathered, router_weight, preferred_element_type=jnp.float32)
     padded = jnp.concatenate([gathered, jnp.zeros((1, gathered.shape[1]), jnp.bfloat16)], axis=0)
     send_rows = padded[inverse].reshape(experts_all, 1, capacity, gathered.shape[1])

time: 210 us -> 210 us (level)
  blocking collectives: 52.6 us -> 31 us
  waiting for transfers between devices: 90.1 us -> 108 us
  starting transfers between devices: 3.48 us -> 6.54 us
    all_gather x1 -> x0, blocking collectives: 21.5 us -> none  [per_device(): gathered = lax.all_gather(tokens, 'hidden', axis=1, tiled=True)]
    ppermute x0 -> x3, waiting for transfers between devices: none -> 18.7 us  [per_device(): lax.ppermute(ring[-1], 'hidden', [(dev, (dev + 1) % 4) for dev in range(4)])]
    ppermute x0 -> x3, starting transfers between devices: none -> 3.06 us  [per_device(): lax.ppermute(ring[-1], 'hidden', [(dev, (dev + 1) % 4) for dev in range(4)])]
  transfers between devices with their start and end apart: 2 -> 5, of which waited for: 2 -> 5; matrix products, arithmetic and copies ran while one was open for 1% -> 3% of each run, Pallas kernels for 0% -> 0%
where the time goes in v1:
time: 210 us
  waiting for transfers between devices  108 us (51%)
  matrix products  35 us (17%)
  blocking collectives  31 us (15%)
  between operations  13.6 us (6%)
  local copies, waits for them, and re-layouts  13.2 us (6%)
  starting transfers between devices  6.54 us (3%)
  other arithmetic  3.11 us (1%)
    reduce_scatter x1, waiting for transfers between devices, per_device(): lax.psum_scatter(partial_value, 'hidden', scatter_dimension=2, tiled=True)  79.6 us
    all_to_all x1, blocking collectives, per_device(): lax.all_to_all(send_rows, 'expert', split_axis=0, concat_axis=1, tiled=True)  31 us
    ppermute x3, waiting for transfers between devices, per_device(): lax.ppermute(ring[-1], 'hidden', [(dev, (dev + 1) % 4) for dev in range(4)])  18.7 us
    dot_general x1, matrix products, per_device(): jnp.einsum('erf,efd->erd', hidden_act, down_weight, preferred_element_typ...  12.9 us
    dot_general x1, matrix products, per_device(): jnp.einsum('ensd,edf->ensf', arrived, up_weight, preferred_element_type=j...  10.9 us
    dot_general x1, matrix products, per_device(): jnp.einsum('ensd,edf->ensf', arrived, gate_weight, preferred_element_type...  10.8 us
    all_to_all x1, waiting for transfers between devices, per_device(): lax.all_to_all(summed, 'expert', split_axis=1, concat_axis=0, tiled=True)  9.45 us
  transfers between devices with their start and end apart: 5, of which 5 were waited for; matrix products, arithmetic and copies ran while one was open for 3% of the time, Pallas kernels for 0%

profile of v1, /device:TPU:0, one launch (start us, length us, event | category | flops | bytes accessed | tf_op | source)
XLA Modules:
  0.0 210.2 jit_solution(17007958677946700056)
XLA Ops:
  6.5 3.1 %collective-permute-start = (bf16[128,768]{1,0:T(8,128)(2,1)}, bf16[128,768]{1,0:T(8,128)(2,1)S(1)}, u32[]{:S(2)}, u32[]{:S(2)}) collective-permute-start(bf16[128,768]{1,0:T(8,128)(2,1)} %param.6), channel_id=1, source_target_pairs={{0,1},{1,2},{2,3},{3,0},{4,5},{5,6},{6,7},{7,4},{8,9},{9,10},{10,1... | collective-permute-start | bytes 589832 | tf_op jit(solution)/shard_map/ppermute | solution.py:25
  9.6 0.8 copy.41
  10.4 0.1 eq.32
  10.5 0.1 eq.28
  10.7 0.6 reduce-window.6
  11.3 0.2 slice_reduce_fusion
  11.6 0.1 reduce_sum.15
  11.9 4.8 %collective-permute-done = bf16[128,768]{1,0:T(8,128)(2,1)S(1)} collective-permute-done((bf16[128,768]{1,0:T(8,128)(2,1)}, bf16[128,768]{1,0:T(8,128)(2,1)S(1)}, u32[]{:S(2)}, u32[]{:S(2)}) %collective-permute-start) | collective-permute-done | bytes 196640 | tf_op jit(solution)/shard_map/ppermute | solution.py:25
  16.8 1.4 scatter_custom_fusion
  18.2 6.5 %collective-permute-done.1 = bf16[128,768]{1,0:T(8,128)(2,1)S(1)} collective-permute-done((bf16[128,768]{1,0:T(8,128)(2,1)S(1)}, bf16[128,768]{1,0:T(8,128)(2,1)S(1)}, u32[]{:S(2)}, u32[]{:S(2)}) %collective-permute-start.1) | collective-permute-done | bytes 196640 | tf_op jit(solution)/shard_map/ppermute | solution.py:25
  24.6 7.5 %collective-permute-done.2 = bf16[128,768]{1,0:T(8,128)(2,1)S(1)} collective-permute-done((bf16[128,768]{1,0:T(8,128)(2,1)S(1)}, bf16[128,768]{1,0:T(8,128)(2,1)S(1)}, u32[]{:S(2)}, u32[]{:S(2)}) %collective-permute-start.2) | collective-permute-done | bytes 196640 | tf_op jit(solution)/shard_map/ppermute | solution.py:25
  32.2 0.9 constant_dynamic-update-slice_fusion.4
  33.2 0.3 constant_dynamic-slice_fusion
  33.5 0.9 copy-done.1
  34.5 2.9 %gather_fusion = bf16[384,3072]{1,0:T(8,128)(2,1)S(1)} fusion(bf16[129,3072]{1,0:T(8,128)(2,1)S(1)} %concatenate.10, s32[1024]{0:T(1024)S(1)} %pad_clamp_fusion.2), kind=kCustom, calls=%fused_computation | custom fusion | bytes 4720128 | tf_op jit(solution)/shard_map/gather | solution.py:33
  37.4 31.0 %all_to_all.33 = bf16[8,1,48,3072]{3,2,1,0:T(8,128)(2,1)S(1)} all-to-all(bf16[8,1,48,3072]{3,2,1,0:T(8,128)(2,1)S(1)} %bitcast.57), channel_id=1, replica_groups=mesh['groups'=2,'expert'=4,'hidden'=4] {'expert'}, dimensions={0} | all-to-all | bytes 4718592 | tf_op jit(solution)/shard_map/all_to_all | solution.py:34
  68.3 10.8 %fusion.2 = f32[2,4,48,2048]{3,2,1,0:T(8,128)S(1)} fusion(bf16[2,3072,2048]{2,1,0:T(8,128)(2,1)} %param.9, bf16[4,2,1,48,3072]{4,3,1,0,2:T(8,128)(2,1)S(1)} %bitcast.52), kind=kOutput, calls=%fused_computation.7 | convolution fusion | flops 4831838208 | bytes 30670848 | tf_op jit(solution)/shard_map/ensd,edf->ensf/dot_general | solution.py:35
  79.1 10.9 %multiply_convert_fusion = bf16[2,4,48,2048]{3,2,1,0:T(8,128)(2,1)S(1)} fusion(f32[2,4,48,2048]{3,2,1,0:T(8,128)S(1)} %fusion.2, bf16[2,3072,2048]{2,1,0:T(8,128)(2,1)} %param.10, bf16[4,2,1,48,3072]{4,3,1,0,2:T(8,128)(2,1)S(1)} %bitcast.53), kind=kOutput, calls=%fused_computation.9 | convolution fusion | flops 4836556800 | bytes 32243712 | tf_op jit(solution)/shard_map/ensd,edf->ensf/dot_general | solution.py:38
  90.1 12.9 %fusion.19 = f32[2,192,3072]{2,1,0:T(8,128)} fusion(bf16[2,192,2048]{2,1,0:T(8,128)(2,1)S(1)} %bitcast.56, bf16[2,2048,3072]{2,1,0:T(8,128)(2,1)} %param.11), kind=kOutput, calls=%fused_computation.54 | convolution fusion | flops 4831838208 | bytes 31457280 | tf_op jit(solution)/shard_map/erf,efd->erd/dot_general | solution.py:41
  103.0 0.7 copy-done.4
  103.8 0.1 reshape.100
  104.0 0.2 fusion.10
  104.2 0.3 fusion.18
  104.5 1.4 gather_fusion.3
  106.1 79.6 %reduce-scatter.2.cloned.1.call-done = f32[2,192,768]{2,1,0:T(8,128)} async-done(((f32[2,192,3072]{2,1,0:T(8,128)}), f32[2,192,768]{2,1,0:T(8,128)}) %reduce-scatter.2.cloned.1.call-update) | async-done | bytes 1179664 | tf_op jit(solution)/shard_map/reduce_scatter | solution.py:44
  185.6 1.3 convert_element_type.25
  187.0 0.8 copy.46
  187.8 3.5 %all-to-all-start.1 = ((bf16[2,4,48,768]{3,2,0,1:T(8,128)(2,1)}), bf16[2,4,48,768]{3,2,0,1:T(8,128)(2,1)S(1)}, u32[]{:S(2)}, u32[]{:S(2)}) async-start(bf16[2,4,48,768]{3,2,0,1:T(8,128)(2,1)} %copy.46), calls=%async_computation.2 | async-start | bytes 1179648 | tf_op jit(solution)/shard_map/all_to_all | solution.py:48
  191.3 9.5 %all-to-all-done.1 = bf16[2,4,48,768]{3,2,0,1:T(8,128)(2,1)S(1)} async-done(((bf16[2,4,48,768]{3,2,0,1:T(8,128)(2,1)}), bf16[2,4,48,768]{3,2,0,1:T(8,128)(2,1)S(1)}, u32[]{:S(2)}, u32[]{:S(2)}) %all-to-all-start.1) | async-done | bytes 589856 | tf_op jit(solution)/shard_map/all_to_all | solution.py:48
  200.8 0.9 gather_fusion.2
  201.7 0.9 gather_fusion.1
  202.5 0.8 add_convert_fusion
  (37 shorter events, 0.9 us)
Async XLA Ops:
  6.5 97.6 %copy-start = (bf16[3072,8]{0,1:T(8,128)(2,1)S(1)}, bf16[3072,8]{0,1:T(8,128)(2,1)}, u32[]{:S(2)}) copy-start(bf16[3072,8]{0,1:T(8,128)(2,1)} %param.8) | copy-start | bytes 147460
  6.5 26.6 %copy-start.3 = (bf16[128,768]{1,0:T(8,128)(2,1)S(1)}, bf16[128,768]{1,0:T(8,128)(2,1)}, u32[]{:S(2)}) copy-start(bf16[128,768]{1,0:T(8,128)(2,1)} %param.6) | copy-start | bytes 589828
  6.5 179.1 %reduce-scatter.2.cloned.1.call-start = ((), (), s32[]{:S(2)}) async-start(), calls=%async_computation.3 | async-start | bytes 5898240 | tf_op jit(solution)/shard_map/reduce_scatter | solution.py:44
  6.5 10.2 %collective-permute-start = (bf16[128,768]{1,0:T(8,128)(2,1)}, bf16[128,768]{1,0:T(8,128)(2,1)S(1)}, u32[]{:S(2)}, u32[]{:S(2)}) collective-permute-start(bf16[128,768]{1,0:T(8,128)(2,1)} %param.6), channel_id=1, source_target_pairs={{0,1},{1,2},{2,3},{3,0},{4,5},{5,6},{6,7},{7,4},{8,9},{9,10},{10,1... | collective-permute-start | bytes 589832 | tf_op jit(solution)/shard_map/ppermute | solution.py:25
  16.8 7.9 %collective-permute-start.1 = (bf16[128,768]{1,0:T(8,128)(2,1)S(1)}, bf16[128,768]{1,0:T(8,128)(2,1)S(1)}, u32[]{:S(2)}, u32[]{:S(2)}) collective-permute-start(bf16[128,768]{1,0:T(8,128)(2,1)S(1)} %collective-permute-done), channel_id=1, source_target_pairs={{0,1},{1,2},{2,3},{3,0},{4,5},{5,6},{6,7},{7,4},{8,9},{9,10},{10,1... | collective-permute-start | bytes 589832 | tf_op jit(solution)/shard_map/ppermute | solution.py:25
  24.6 7.5 %collective-permute-start.2 = (bf16[128,768]{1,0:T(8,128)(2,1)S(1)}, bf16[128,768]{1,0:T(8,128)(2,1)S(1)}, u32[]{:S(2)}, u32[]{:S(2)}) collective-permute-start(bf16[128,768]{1,0:T(8,128)(2,1)S(1)} %collective-permute-done.1), channel_id=1, source_target_pairs={{0,1},{1,2},{2,3},{3,0},{4,5},{5,6},{6,7},{7,4},{8,9},{9,10},{10,1... | collective-permute-start | bytes 589832 | tf_op jit(solution)/shard_map/ppermute | solution.py:25
  33.5 0.9 copy-start.1
  103.0 0.7 copy-start.4
  103.0 1.2 copy-start.2
  187.8 13.0 %all-to-all-start.1 = ((bf16[2,4,48,768]{3,2,0,1:T(8,128)(2,1)}), bf16[2,4,48,768]{3,2,0,1:T(8,128)(2,1)S(1)}, u32[]{:S(2)}, u32[]{:S(2)}) async-start(bf16[2,4,48,768]{3,2,0,1:T(8,128)(2,1)} %copy.46), calls=%async_computation.2 | async-start | bytes 1179648 | tf_op jit(solution)/shard_map/all_to_all | solution.py:48
Sparse Core Ops, SparseCore 0:
  103.2 82.4 reduce-scatter.1
